TPU v7x, 512 devices: a whole 4x8x8 slice. The times are simulated.
512 devices in a mesh: section: 8 (over x, core), expert: 64 (over z, y).
Axes of the slice: x: 4, y: 8, z: 8, core: 2. Of those that a mesh axis runs over, the one named last changes fastest.
Arguments:
- x_fwd: bfloat16 [8, 8192, 3584], P('section', 'expert'), may hold values from -6 to 6
- routes_fwd: int32 [8, 8192, 8], P('section', 'expert'), may hold values from 0 to 255, as said below
- gates_fwd: float32 [8, 8192, 8], P('section', 'expert'), may hold values from 0.1 to 0.6
- w_gate: bfloat16 [8, 64, 3584, 128], P('section', 'expert'), may hold values from -0.09375 to 0.09375
- w_up: bfloat16 [8, 64, 3584, 128], P('section', 'expert'), may hold values from -0.09375 to 0.09375
- w_down: bfloat16 [8, 64, 128, 3584], P('section', 'expert'), may hold values from -0.1875 to 0.1875
Outputs:
- act_next: bfloat16 [8, 8192, 3584], P('section', 'expert')
Inputs may be any that keep to these rules, and one draw needn't show every extreme that they name: `routes_fwd`: the 8 experts of a token differ. Within the rows of one device no expert below 8 is chosen by more than 10 tokens, and in every draw one such expert is chosen by exactly 10 tokens of every device.
All inputs are finite; a program needn't handle non-finite values.
Results may differ from a plain program's by a relative error of at most 0.0024.
Values may be sent and summed in bfloat16 or wider, within the bound.
No kernel may reach another device: no remote copies, remote signals or barrier semaphores. Data moves between devices by JAX's collectives and lax.ppermute only.
A program may use at most 64 MiB of HBM per device.

v0:
```python
import jax
import jax.numpy as jnp
from jax import lax
from jax.sharding import PartitionSpec as P

HID = 1024
H_DEV = 128
CAP = 10


def passed_along(value, axis, steps):
    count = lax.axis_size(axis)
    initial, last = (max(0, -steps), min(count, count - steps))
    return lax.ppermute(value, axis, [(source, source + steps) for source in range(initial, last)])


def positions(routes, count):
    flat = routes.reshape(-1)
    onehot = (flat[:, None] == jnp.arange(count, dtype=jnp.int32)[None, :]).astype(jnp.int32)
    before = jnp.cumsum(onehot, axis=0) - onehot
    return jnp.sum(onehot * before, axis=1).reshape(routes.shape)


def slot_index(routes, live, capacity):
    placed = positions(routes, live)
    return jnp.where(routes < live, routes * capacity + placed, live * capacity)


def block_forward(rows, wg, wu, wd):
    pre_gate = jnp.dot(rows, wg, preferred_element_type=jnp.float32)
    pre_up = jnp.dot(rows, wu, preferred_element_type=jnp.float32)
    act = (pre_gate * jax.nn.sigmoid(pre_gate) * pre_up).astype(jnp.bfloat16)
    return jnp.dot(act, wd, preferred_element_type=jnp.float32).astype(jnp.bfloat16)


def place_rows(rows, index, live, capacity):
    slot_ids = jnp.arange(live * capacity, dtype=jnp.int32)
    match = jnp.any(index[None, :, :] == slot_ids[:, None, None], axis=2).astype(jnp.bfloat16)
    placed = jnp.dot(match, rows, preferred_element_type=jnp.float32).astype(jnp.bfloat16)
    return placed.reshape(live, capacity, rows.shape[1])


def shards(x_fwd, routes_fwd, gates_fwd, w_gate, w_up, w_down):
    devices_here = lax.axis_size("expert")
    group = HID // H_DEV
    live = devices_here // group
    capacity = CAP
    x_a = x_fwd[0]
    gate_a = gates_fwd[0]
    depth = x_a.shape[1]
    wg = w_gate[0, 0]
    wu = w_up[0, 0]
    wd = w_down[0, 0]
    index_a = slot_index(routes_fwd[0], live, capacity)
    placed = place_rows(x_a, index_a, live, capacity)
    send_a = jnp.repeat(placed, group, axis=0)
    received = lax.all_to_all(send_a, "expert", split_axis=0, concat_axis=0, tiled=True)
    count, items, width = received.shape
    outs_a = block_forward(received.reshape(count * items, width), wg, wu, wd).reshape(
        count, items, width
    )
    back_a = lax.all_to_all(outs_a, "expert", split_axis=0, concat_axis=0, tiled=True)
    summed = jnp.sum(back_a.reshape(live, group, capacity, depth), axis=1, dtype=jnp.float32)
    summed = summed.reshape(live * capacity, depth)
    slot_ids = jnp.arange(live * capacity, dtype=jnp.int32)
    weights = jnp.sum(
        jnp.where(index_a[:, :, None] == slot_ids[None, None, :], gate_a[:, :, None], 0.0), axis=1
    )
    layer_out = x_a.astype(jnp.float32) + jnp.dot(weights, summed, precision=lax.Precision.HIGHEST)
    act_next = passed_along(layer_out.astype(jnp.bfloat16), "section", 1)
    return act_next[None]


def solution(mesh):
    in_specs = (
        P("section", "expert", None),
        P("section", "expert", None),
        P("section", "expert", None),
        P("section", "expert", None, None),
        P("section", "expert", None, None),
        P("section", "expert", None, None),
    )
    out_specs = P("section", "expert", None)
    return jax.shard_map(shards, mesh=mesh, in_specs=in_specs, out_specs=out_specs, check_vma=False)
```

profile of v0, /device:TPU:114, one launch (start us, length us, event | category | flops | bytes accessed | tf_op | source)
XLA Modules:
  0.0 498.2 jit_solution(8583310920082393275)
XLA Ops:
  0.0 0.0 copy-start
  0.0 0.9 copy.15
  0.9 0.1 eq.57
  1.0 0.1 eq.53
  1.1 2.3 reduce-window.6
  3.3 0.3 slice_reduce_fusion
  3.6 0.2 reduce-window.9
  3.8 0.1 add_bitcast_fusion
  3.9 0.1 reshape.63
  4.1 0.1 fusion.13
  4.2 1.5 convolution_convert_fusion.1
  5.7 0.2 reshape.64
  5.9 0.9 broadcast_in_dim.36
  6.8 181.3 %all_to_all.10 = bf16[64,10,3584]{2,1,0:T(8,128)(2,1)} all-to-all(bf16[64,10,3584]{2,1,0:T(8,128)(2,1)S(1)} %bitcast.52), channel_id=1, replica_groups=mesh['section'=8,'expert'=64] {'expert'}, dimensions={0} | all-to-all | bytes 9175040 | tf_op jit(solution)/shard_map/all_to_all | solution.py:57
  188.1 0.0 copy-start.3
  188.1 8.1 %reshape.66 = bf16[640,3584]{1,0:T(8,128)(2,1)} reshape(bf16[64,10,3584]{2,1,0:T(8,128)(2,1)} %all_to_all.10) | data formatting | bytes 9175040 | tf_op jit(solution)/shard_map/reshape | solution.py:59
  196.2 0.0 copy-done.3
  196.2 0.0 copy-start.1
  196.2 3.7 fusion.5
  199.9 0.0 copy-done
  199.9 0.0 copy-done.1
  199.9 9.3 %convolution_convert_fusion = bf16[640,3584]{1,0:T(8,128)(2,1)} fusion(bf16[640,3584]{1,0:T(8,128)(2,1)} %reshape.66, bf16[1,1,128,3584]{3,2,1,0:T(8,128)(2,1)S(1)} %copy-done, bf16[1,1,3584,128]{3,2,1,0:T(8,128)(2,1)S(1)} %copy-done.1, f32[640,128]{1,0:T(8,128)S(1)} %fusion.5), kind=kOutput, calls=%fused_computation.1 | convolution fusion | flops 1177190400 | bytes 11337728 | tf_op jit(solution)/shard_map/dot_general | solution.py:33
  209.2 7.7 %reshape.67 = bf16[64,10,3584]{2,1,0:T(8,128)(2,1)} reshape(bf16[640,3584]{1,0:T(8,128)(2,1)} %convolution_convert_fusion) | data formatting | bytes 9175040 | tf_op jit(solution)/shard_map/reshape | solution.py:59
  216.9 0.0 copy-start.2
  216.9 16.3 %all-to-all-start.1 = ((bf16[64,10,3584]{2,1,0:T(8,128)(2,1)}), bf16[64,10,3584]{2,1,0:T(8,128)(2,1)}, u32[]{:S(2)}, u32[]{:S(2)}) async-start(bf16[64,10,3584]{2,1,0:T(8,128)(2,1)} %reshape.67), calls=%async_computation.1 | async-start | bytes 14680064 | tf_op jit(solution)/shard_map/all_to_all | solution.py:62
  233.3 0.1 reshape.62
  233.4 0.0 copy-done.2
  233.5 0.1 select_reduce_fusion
  233.5 240.0 %all-to-all-done.1 = bf16[64,10,3584]{2,1,0:T(8,128)(2,1)} async-done(((bf16[64,10,3584]{2,1,0:T(8,128)(2,1)}), bf16[64,10,3584]{2,1,0:T(8,128)(2,1)}, u32[]{:S(2)}, u32[]{:S(2)}) %all-to-all-start.1) | async-done | bytes 4587552 | tf_op jit(solution)/shard_map/all_to_all | solution.py:62
  473.6 4.6 convert_reduce_fusion
  478.2 1.2 reshape.68
  479.3 3.2 fusion
  482.5 1.9 collective-permute-start
  484.5 12.8 %collective-permute-done = bf16[128,3584]{1,0:T(8,128)(2,1)S(1)} collective-permute-done((bf16[128,3584]{1,0:T(8,128)(2,1)S(1)}, bf16[128,3584]{1,0:T(8,128)(2,1)S(1)}, u32[]{:S(2)}, u32[]{:S(2)}) %collective-permute-start) | collective-permute-done | bytes 917536 | tf_op jit(solution)/shard_map/ppermute | solution.py:14
  497.3 0.9 copy.24
  (6 shorter events, 0.2 us)
Async XLA Ops:
  0.0 199.9 %copy-start = (bf16[1,1,128,3584]{3,2,1,0:T(8,128)(2,1)S(1)}, bf16[1,1,128,3584]{3,2,1,0:T(8,128)(2,1)}, u32[]{:S(2)}) copy-start(bf16[1,1,128,3584]{3,2,1,0:T(8,128)(2,1)} %param.11) | copy-start | bytes 2752516
  188.1 8.1 %copy-start.3 = (bf16[1,1,3584,128]{3,2,1,0:T(8,128)(2,1)S(1)}, bf16[1,1,3584,128]{3,2,1,0:T(8,128)(2,1)}, u32[]{:S(2)}) copy-start(bf16[1,1,3584,128]{3,2,1,0:T(8,128)(2,1)} %param.9) | copy-start | bytes 2752516
  196.2 3.7 copy-start.1
  216.9 16.5 %copy-start.2 = (f32[1,128,8]{1,2,0:T(8,128)S(1)}, f32[1,128,8]{1,2,0:T(8,128)}, u32[]{:S(2)}) copy-start(f32[1,128,8]{1,2,0:T(8,128)} %param.8) | copy-start | bytes 12292
  216.9 256.6 %all-to-all-start.1 = ((bf16[64,10,3584]{2,1,0:T(8,128)(2,1)}), bf16[64,10,3584]{2,1,0:T(8,128)(2,1)}, u32[]{:S(2)}, u32[]{:S(2)}) async-start(bf16[64,10,3584]{2,1,0:T(8,128)(2,1)} %reshape.67), calls=%async_computation.1 | async-start | bytes 14680064 | tf_op jit(solution)/shard_map/all_to_all | solution.py:62
  482.5 14.7 %collective-permute-start = (bf16[128,3584]{1,0:T(8,128)(2,1)S(1)}, bf16[128,3584]{1,0:T(8,128)(2,1)S(1)}, u32[]{:S(2)}, u32[]{:S(2)}) collective-permute-start(bf16[128,3584]{1,0:T(8,128)(2,1)S(1)} %fusion), channel_id=1, source_target_pairs={{0,64},{64,128},{128,192},{192,256},{256,320},{320,384},{384,448},... | collective-permute-start | bytes 2752520 | tf_op jit(solution)/shard_map/ppermute | solution.py:14
where the time goes:
time: 499 us; the launch traced here: 498 us
  waiting for transfers between devices  253 us (51%)
  blocking collectives  181 us (36%)
  local copies, waits for them, and re-layouts  20.5 us (4%)
  starting transfers between devices  18.3 us (4%)
  matrix products  17.8 us (4%)
  other arithmetic  7.36 us (1%)
    all_to_all x1, waiting for transfers between devices, shards(): lax.all_to_all(outs_a, 'expert', split_axis=0, concat_axis=0, tiled=True)  240 us
    all_to_all x1, blocking collectives, shards(): lax.all_to_all(send_a, 'expert', split_axis=0, concat_axis=0, tiled=True)  181 us
    all_to_all x1, starting transfers between devices, shards(): lax.all_to_all(outs_a, 'expert', split_axis=0, concat_axis=0, tiled=True)  16.3 us
    ppermute x1, waiting for transfers between devices, passed_along(): lax.ppermute(value, axis, [(source, source + steps) for source in range(i...  12.8 us
  transfers between devices with their start and end apart: 2, of which 2 were waited for; matrix products, arithmetic and copies ran while one was open for 0% of the time, Pallas kernels for 0%

commit v1 on v0

v1 whole, which is shorter than its diff:
```python
import functools

import jax
import jax.numpy as jnp
from jax import lax
from jax.experimental import pallas as pl
from jax.experimental.pallas import tpu as pltpu
from jax.sharding import Mesh, PartitionSpec as P

CAP = 10
LIVE = 8
PIECES = 4
BLOCK = CAP * PIECES
ROWS = LIVE * CAP
PLACED = LIVE * BLOCK

F32 = jnp.float32
BF16 = jnp.bfloat16


def iota(shape, dim):
    return lax.broadcasted_iota(jnp.int32, shape, dim)


def slot_keys(routes_t):
    tokens = routes_t.shape[1]
    hit = jnp.concatenate(
        [jnp.max((routes_t == e).astype(F32), axis=0, keepdims=True) for e in range(LIVE)], axis=0
    )
    earlier = (iota((tokens, tokens), 0) < iota((tokens, tokens), 1)).astype(BF16)
    rank = jnp.dot(hit.astype(BF16), earlier, preferred_element_type=F32)
    return jnp.where(hit > 0, rank, -1.0)


def spread(values):
    pick = (iota((PLACED, LIVE), 0) // BLOCK == iota((PLACED, LIVE), 1)).astype(BF16)
    return jnp.dot(pick, values, preferred_element_type=F32)


def slot_match(routes_t):
    keys = spread(slot_keys(routes_t).astype(BF16))
    slots = (iota(keys.shape, 0) % CAP).astype(F32)
    return keys == slots


def piece_of(shape):
    return iota(shape, 0) // CAP % PIECES


def place_kernel(routes_ref, x_ref, out_ref):
    match = slot_match(routes_ref[...])
    piece = piece_of(match.shape)
    width = x_ref.shape[1] // PIECES
    total = jnp.zeros(out_ref.shape, F32)
    for p in range(PIECES):
        one = jnp.where(match & (piece == p), 1.0, 0.0).astype(BF16)
        total += jnp.dot(one, x_ref[:, p * width:(p + 1) * width], preferred_element_type=F32)
    out_ref[...] = total.astype(BF16)


def whole_rows_kernel(in_ref, out_ref):
    width = in_ref.shape[1]
    row, col = iota((ROWS, PLACED), 0), iota((ROWS, PLACED), 1)
    same = (row // CAP == col // BLOCK) & (row % CAP == col % CAP)
    for p in range(PIECES):
        one = jnp.where(same & (col // CAP % PIECES == p), 1.0, 0.0).astype(BF16)
        moved = jnp.dot(one, in_ref[...], preferred_element_type=F32)
        out_ref[:, p * width:(p + 1) * width] = moved.astype(BF16)


def pieces_kernel(in_ref, out_ref):
    width = out_ref.shape[1]
    row, col = iota((PLACED, ROWS), 0), iota((PLACED, ROWS), 1)
    same = (col // CAP == row // BLOCK) & (col % CAP == row % CAP)
    total = jnp.zeros(out_ref.shape, F32)
    for p in range(PIECES):
        one = jnp.where(same & (row // CAP % PIECES == p), 1.0, 0.0).astype(BF16)
        total += jnp.dot(one, in_ref[:, p * width:(p + 1) * width], preferred_element_type=F32)
    out_ref[...] = total.astype(BF16)


def expert_kernel(rows_ref, wg_ref, wu_ref, wd_ref, out_ref, both_ref):
    hid = wg_ref.shape[1]

    @pl.when(pl.program_id(0) == 0)
    def _():
        both_ref[:, :hid] = wg_ref[...]
        both_ref[:, hid:] = wu_ref[...]

    pre = jnp.dot(rows_ref[...], both_ref[...], preferred_element_type=F32)
    gate, up = pre[:, :hid], pre[:, hid:]
    act = (gate * jax.nn.sigmoid(gate) * up).astype(BF16)
    out_ref[...] = jnp.dot(act, wd_ref[...], preferred_element_type=F32).astype(BF16)


def combine_kernel(routes_ref, gates_ref, x_ref, back_ref, out_ref):
    routes = routes_ref[...]
    match = slot_match(routes)
    gates = gates_ref[...]
    rows = [
        jnp.sum(jnp.where(routes == e, gates, 0.0), axis=0, keepdims=True) for e in range(LIVE)
    ]
    left = jnp.concatenate(rows, axis=0)
    terms = []
    for _ in range(3):
        term = left.astype(BF16)
        left = left - term.astype(F32)
        terms.append(jnp.where(match, spread(term), 0.0).astype(BF16))
    piece = piece_of(match.shape)
    width = back_ref.shape[1]
    back = back_ref[...]
    over_rows = (((0,), (0,)), ((), ()))
    for p in range(PIECES):
        here = piece == p
        total = x_ref[:, p * width:(p + 1) * width].astype(F32)
        for term in terms:
            one = jnp.where(here, term, jnp.zeros_like(term))
            total += lax.dot_general(one, back, over_rows, preferred_element_type=F32)
        out_ref[:, p * width:(p + 1) * width] = total.astype(BF16)


def whole(kernel, shape, *args):
    return pl.pallas_call(kernel, out_shape=jax.ShapeDtypeStruct(shape, BF16))(*args)


def expert_block(rows, wg, wu, wd):
    count, depth = rows.shape
    hid = wg.shape[1]
    tile = 128
    fixed = functools.partial(pl.BlockSpec, index_map=lambda i: (0, 0))
    return pl.pallas_call(
        expert_kernel,
        grid=(count // tile,),
        in_specs=[
            pl.BlockSpec((tile, depth), lambda i: (i, 0)),
            fixed((depth, hid)),
            fixed((depth, hid)),
            fixed((hid, depth)),
        ],
        out_specs=pl.BlockSpec((tile, depth), lambda i: (i, 0)),
        out_shape=jax.ShapeDtypeStruct((count, depth), BF16),
        scratch_shapes=[pltpu.VMEM((depth, 2 * hid), BF16)],
    )(rows, wg, wu, wd)


def shards(x_fwd, routes_fwd, gates_fwd, w_gate, w_up, w_down):
    x = x_fwd[0]
    routes_t, gates_t = routes_fwd[0].T, gates_fwd[0].T
    depth = x.shape[1]
    width = depth // PIECES
    placed = whole(place_kernel, (PLACED, width), routes_t, x)
    arrived = lax.all_to_all(placed.reshape(LIVE, BLOCK, width), "z", 0, 0, tiled=True)
    rows = whole(whole_rows_kernel, (ROWS, depth), arrived.reshape(PLACED, width))
    rows = lax.all_gather(rows, "y", axis=0, tiled=True)
    parts = expert_block(rows, w_gate[0, 0], w_up[0, 0], w_down[0, 0])
    summed = lax.psum_scatter(parts, "y", scatter_dimension=0, tiled=True)
    summed = whole(pieces_kernel, (PLACED, width), summed)
    back = lax.all_to_all(summed.reshape(LIVE, BLOCK, width), "z", 0, 0, tiled=True)
    y = whole(combine_kernel, x.shape, routes_t, gates_t, x, back.reshape(PLACED, width))
    sections = lax.axis_size("section")
    return lax.ppermute(y, "section", [(s, s + 1) for s in range(sections - 1)])[None]


def solution(mesh):
    sections, experts = mesh.devices.shape
    grid = Mesh(mesh.devices.reshape(sections, LIVE, experts // LIVE), ("section", "z", "y"))
    three = P("section", ("z", "y"), None)
    four = P("section", ("z", "y"), None, None)
    return jax.shard_map(
        shards,
        mesh=grid,
        in_specs=(three, three, three, four, four, four),
        out_specs=three,
        check_vma=False,
    )
```

time: 499 us -> 225 us (0.45)
  the two profiles are of different devices: /device:TPU:114 before, /device:TPU:1 now
where the time goes in v1:
time: 225 us; the launch traced here: 224 us
  waiting for transfers between devices  130 us (58%)
  blocking collectives  51.9 us (23%)
  Pallas kernels  22.5 us (10%)
  between operations  13.4 us (6%)
  starting transfers between devices  5.71 us (3%)
    reduce_scatter x1, waiting for transfers between devices, shards(): summed = lax.psum_scatter(parts, 'y', scatter_dimension=0, tiled=True)  60.7 us
    all_gather x1, waiting for transfers between devices, shards(): rows = lax.all_gather(rows, 'y', axis=0, tiled=True)  58.7 us
    all_to_all x1, blocking collectives, shards(): lax.all_to_all(placed.reshape(LIVE, BLOCK, width), 'z', 0, 0, tiled=True)  27.9 us
    all_to_all x1, blocking collectives, shards(): lax.all_to_all(summed.reshape(LIVE, BLOCK, width), 'z', 0, 0, tiled=True)  24 us
    pallas_call x4, Pallas kernels, whole(): pl.pallas_call(kernel, out_shape=jax.ShapeDtypeStruct(shape, BF16))(*args)  12.6 us
    ppermute x1, waiting for transfers between devices, shards(): lax.ppermute(y, 'section', [(s, s + 1) for s in range(sections - 1)])[None]  10.6 us
    pallas_call x1, Pallas kernels, expert_block(): pl.pallas_call(expert_kernel, grid=(count // tile,), in_specs=[pl.BlockSp...  9.88 us
    ppermute x1, starting transfers between devices, shards(): lax.ppermute(y, 'section', [(s, s + 1) for s in range(sections - 1)])[None]  5.67 us
  transfers between devices with their start and end apart: 3, of which 3 were waited for; matrix products, arithmetic and copies ran while one was open for 0% of the time, Pallas kernels for 0%

profile of v1, /device:TPU:1, one launch (start us, length us, event | category | flops | bytes accessed | tf_op | source)
XLA Modules:
  0.0 224.5 jit_solution(5957688056512692540)
XLA Ops:
  6.5 0.0 all-gather.2.cloned.1.call-start
  6.5 3.0 %shard_map.64 = bf16[320,896]{1,0:T(8,128)(2,1)} custom-call(s32[8,128]{1,0:T(8,128)} %bitcast.25, bf16[128,3584]{1,0:T(8,128)(2,1)} %bitcast.15), custom_call_target="tpu_custom_call" | custom-call | tf_op jit(solution)/shard_map/pallas_call | solution.py:123
  9.5 27.9 %all_to_all.10 = bf16[8,40,896]{2,1,0:T(8,128)(2,1)} all-to-all(bf16[8,40,896]{2,1,0:T(8,128)(2,1)} %bitcast.20), channel_id=1, replica_groups=mesh['section'=8,'z'=8,'y'=8] {'z'}, dimensions={0} | all-to-all | bytes 1146880 | tf_op jit(solution)/shard_map/all_to_all | solution.py:152
  37.5 2.5 %shard_map.65 = bf16[80,3584]{1,0:T(8,128)(2,1)} custom-call(bf16[320,896]{1,0:T(8,128)(2,1)} %bitcast.18), custom_call_target="tpu_custom_call" | custom-call | tf_op jit(solution)/shard_map/pallas_call | solution.py:123
  39.9 0.0 all-gather.2.cloned.1.call-update
  40.0 0.0 reduce-scatter.2.cloned.1.call-start
  40.0 58.7 %all-gather.2.cloned.1.call-done.rows_ref = bf16[640,3584]{1,0:T(8,128)(2,1)} async-done(((bf16[80,3584]{1,0:T(8,128)(2,1)}), bf16[640,3584]{1,0:T(8,128)(2,1)}) %all-gather.2.cloned.1.call-update) | async-done | bytes 4587536 | tf_op jit(solution)/shard_map/all_gather | solution.py:154
  98.7 9.9 %shard_map.66 = bf16[640,3584]{1,0:T(8,128)(2,1)} custom-call(bf16[640,3584]{1,0:T(8,128)(2,1)} %all-gather.2.cloned.1.call-done.rows_ref, bf16[3584,128]{1,0:T(8,128)(2,1)} %bitcast.21, bf16[3584,128]{1,0:T(8,128)(2,1)} %bitcast.22, bf16[128,3584]{1,0:T(8,128)(2,1)} %bitcast.23), custom_call_target="tpu_custom_call" | custom-call | tf_op jit(solution)/shard_map/pallas_call | solution.py:131
  108.6 0.0 reduce-scatter.2.cloned.1.call-update
  108.6 60.7 %reduce-scatter.2.cloned.1.call-done.in_ref = bf16[80,3584]{1,0:T(8,128)(2,1)} async-done(((bf16[640,3584]{1,0:T(8,128)(2,1)}), bf16[80,3584]{1,0:T(8,128)(2,1)}) %reduce-scatter.2.cloned.1.call-update) | async-done | bytes 573456 | tf_op jit(solution)/shard_map/reduce_scatter | solution.py:156
  169.3 2.7 %shard_map.67 = bf16[320,896]{1,0:T(8,128)(2,1)} custom-call(bf16[80,3584]{1,0:T(8,128)(2,1)} %reduce-scatter.2.cloned.1.call-done.in_ref), custom_call_target="tpu_custom_call" | custom-call | tf_op jit(solution)/shard_map/pallas_call | solution.py:123
  172.0 24.0 %all_to_all.11 = bf16[8,40,896]{2,1,0:T(8,128)(2,1)} all-to-all(bf16[8,40,896]{2,1,0:T(8,128)(2,1)} %bitcast.19), channel_id=1, replica_groups=mesh['section'=8,'z'=8,'y'=8] {'z'}, dimensions={0} | all-to-all | bytes 1146880 | tf_op jit(solution)/shard_map/all_to_all | solution.py:158
  196.0 4.5 %shard_map.68 = bf16[128,3584]{1,0:T(8,128)(2,1)} custom-call(s32[8,128]{1,0:T(8,128)} %bitcast.26, f32[8,128]{1,0:T(8,128)} %bitcast.27, bf16[128,3584]{1,0:T(8,128)(2,1)} %bitcast.16, bf16[320,896]{1,0:T(8,128)(2,1)} %bitcast.17), custom_call_target="tpu_custom_call" | custom-call | tf_op jit(solution)/shard_map/pallas_call | solution.py:123
  200.4 5.7 %collective-permute-start = (bf16[128,3584]{1,0:T(8,128)(2,1)}, bf16[128,3584]{1,0:T(8,128)(2,1)S(1)}, u32[]{:S(2)}, u32[]{:S(2)}) collective-permute-start(bf16[128,3584]{1,0:T(8,128)(2,1)} %shard_map.68), channel_id=1, source_target_pairs={{0,64},{64,128},{128,192},{192,256},{256,320},{320,384},{384,448},... | collective-permute-start | bytes 2752520 | tf_op jit(solution)/shard_map/ppermute | solution.py:161
  206.1 10.6 %collective-permute-done = bf16[128,3584]{1,0:T(8,128)(2,1)S(1)} collective-permute-done((bf16[128,3584]{1,0:T(8,128)(2,1)}, bf16[128,3584]{1,0:T(8,128)(2,1)S(1)}, u32[]{:S(2)}, u32[]{:S(2)}) %collective-permute-start) | collective-permute-done | bytes 917536 | tf_op jit(solution)/shard_map/ppermute | solution.py:161
  216.7 0.9 copy.8
Async XLA Ops:
  6.5 92.2 %all-gather.2.cloned.1.call-start = ((), (), s32[]{:S(2)}) async-start(), calls=%async_computation.3 | async-start | bytes 5160960 | tf_op jit(solution)/shard_map/all_gather | solution.py:154
  40.0 129.3 %reduce-scatter.2.cloned.1.call-start = ((), (), s32[]{:S(2)}) async-start(), calls=%async_computation.4 | async-start | bytes 5160960 | tf_op jit(solution)/shard_map/reduce_scatter | solution.py:156
  200.4 16.3 %collective-permute-start = (bf16[128,3584]{1,0:T(8,128)(2,1)}, bf16[128,3584]{1,0:T(8,128)(2,1)S(1)}, u32[]{:S(2)}, u32[]{:S(2)}) collective-permute-start(bf16[128,3584]{1,0:T(8,128)(2,1)} %shard_map.68), channel_id=1, source_target_pairs={{0,64},{64,128},{128,192},{192,256},{256,320},{320,384},{384,448},... | collective-permute-start | bytes 2752520 | tf_op jit(solution)/shard_map/ppermute | solution.py:161
Sparse Core Ops, SparseCore 0:
  40.1 58.5 all-gather.1
  108.7 60.4 reduce-scatter.1
